TPU v7x, 512 devices: a whole 4x4x16 slice. The times are simulated.
512 devices in a mesh: rows: 128 (over z, y, core), cols: 4 (over x).
Axes of the slice: x: 4, y: 4, z: 16, core: 2. Of those that a mesh axis runs over, the one named last changes fastest.
Arguments:
- embeddings: bfloat16 [131072, 1024], P('rows'), may hold values from -6 to 6
- knn_mean: bfloat16 [131072], P('rows'), may hold values from 0.29882812 to 0.8984375
- pair_rows: int32 [128, 4, 24], P('rows', 'cols'), may hold values from 0 to 511, as said below
- pair_cols: int32 [128, 4, 24], P('rows', 'cols'), may hold values from 0 to 511, as said below
- pair_count: int32 [128, 4], P('rows', 'cols'), may hold values from 2 to 24, as said below
- start_block: float32 [64, 131072], P(None, 'rows')
Outputs:
- block_vector: float32 [64, 131072], P(None, 'rows')
Inputs may be any that keep to these rules, and one draw needn't show every extreme that they name: `pair_count`: on every index of rows one device of cols has exactly 24 live slots. `pair_rows`: A live entry of device (i, j) is one of the row blocks i * 4 to (i + 1) * 4 - 1; the live pairs of one index of rows are all different, and each of its row blocks is paired with itself. Slots at pair_count and beyond are unused and repeat the device's first pair. `pair_cols`: the column block of a live pair of device (i, j) is a row block of rows index i - 1, i or i + 1.
All inputs are finite; a program needn't handle non-finite values.
Results may differ from a plain program's by a relative error of at most 0.0065.
Values may be sent and summed in bfloat16 or wider, within the bound.
A program may use at most 64 MiB of HBM per device.

v0:
```python
import math

import jax
import jax.numpy as jnp
from jax import lax
from jax.sharding import PartitionSpec as P

K = 64
BLOCK = 256
ITERS = 2


sharpness = 10.0
epsilon = 1e-06


def extended(cells, sides, width):
    for axis, dim in sides:
        count = lax.axis_size(axis)
        ends = count - 1
        head = lax.slice_in_dim(cells, 0, width, axis=dim)
        tail = lax.slice_in_dim(cells, cells.shape[dim] - width, cells.shape[dim], axis=dim)
        cells = jnp.concatenate(
            [
                lax.ppermute(tail, axis, [(i, (i + 1) % count) for i in range(ends)]),
                cells,
                lax.ppermute(head, axis, [((i + 1) % count, i) for i in range(ends)]),
            ],
            axis=dim,
        )
    return cells


def unit_rows(embeddings):
    values = embeddings.astype(jnp.float32)
    scale = lax.rsqrt(jnp.mean(values * values, axis=1, keepdims=True) + epsilon)
    return (values * scale / math.sqrt(values.shape[1])).astype(jnp.bfloat16)


def make_affinity(row_unit, col_unit, row_mean, col_mean, row_block, col_block):
    size = row_unit.shape[0]
    scores = lax.dot_general(
        row_unit, col_unit, (((1,), (1,)), ((), ())), preferred_element_type=jnp.float32
    )
    denom = 0.5 * (row_mean.astype(jnp.float32)[:, None] + col_mean.astype(jnp.float32)[None, :])
    weights = jnp.exp(sharpness * scores / denom)
    offsets = jnp.arange(size, dtype=jnp.int32)
    same = (row_block * size + offsets)[:, None] == (col_block * size + offsets)[None, :]
    return jnp.where(same, jnp.zeros_like(weights), weights).astype(jnp.bfloat16)


def add_block(accum, piece, block_index):
    size = piece.shape[1]
    current = lax.dynamic_slice_in_dim(accum, block_index * size, size, 1)
    return lax.dynamic_update_slice_in_dim(accum, current + piece, block_index * size, 1)


def local(embeddings, knn_mean, pair_rows, pair_cols, pair_count, start_block):
    rows_here = embeddings.shape[0]
    blocks_here = rows_here // BLOCK
    slots = pair_rows.shape[2]
    group_index = lax.axis_index("rows")
    total_rows = rows_here * lax.axis_size("rows")
    unit = unit_rows(embeddings)
    window_unit, window_mean = (
        extended(unit, (("rows", 0),), rows_here),
        extended(knn_mean, (("rows", 0),), rows_here),
    )
    my_rows = pair_rows.reshape(-1)
    my_cols = pair_cols.reshape(-1)
    live_count = pair_count.reshape(())
    local_rows = my_rows - group_index * blocks_here
    window_cols = my_cols - (group_index - 1) * blocks_here
    cache = jnp.zeros((slots, BLOCK, BLOCK), jnp.bfloat16)
    degree_part = jnp.zeros((1, rows_here), jnp.float32)
    vector = start_block
    for sweep in range(ITERS):
        narrow = extended(vector.astype(jnp.bfloat16), (("rows", 1),), rows_here)

        def accumulate(slot, state):
            vector_acc, degree_acc, stored = state
            row_block = local_rows[slot]
            col_block = window_cols[slot]
            if sweep == 0:
                row_unit = lax.dynamic_slice_in_dim(
                    window_unit, (blocks_here + row_block) * BLOCK, BLOCK, 0
                )
                col_unit = lax.dynamic_slice_in_dim(window_unit, col_block * BLOCK, BLOCK, 0)
                row_mean = lax.dynamic_slice_in_dim(
                    window_mean, (blocks_here + row_block) * BLOCK, BLOCK, 0
                )
                col_mean = lax.dynamic_slice_in_dim(window_mean, col_block * BLOCK, BLOCK, 0)
                affinity = make_affinity(
                    row_unit, col_unit, row_mean, col_mean, my_rows[slot], my_cols[slot]
                )
                stored = lax.dynamic_update_index_in_dim(stored, affinity, slot, 0)
                degree_acc = add_block(
                    degree_acc, jnp.sum(affinity.astype(jnp.float32), axis=1)[None, :], row_block
                )
            else:
                affinity = lax.dynamic_index_in_dim(stored, slot, 0, keepdims=False)
            source = lax.dynamic_slice_in_dim(narrow, col_block * BLOCK, BLOCK, 1)
            product = lax.dot_general(
                source, affinity, (((1,), (1,)), ((), ())), preferred_element_type=jnp.float32
            )
            vector_acc = add_block(vector_acc, product, row_block)
            return (vector_acc, degree_acc, stored)

        start_state = (jnp.zeros((K, rows_here), jnp.float32), degree_part, cache)
        partial_value, degree_part, cache = lax.fori_loop(0, live_count, accumulate, start_state)
        summed, degree = lax.psum((partial_value, degree_part), "cols")
        smoothed = summed / degree
        gram = (
            jnp.dot(
                smoothed,
                smoothed.T,
                precision=lax.Precision.HIGHEST,
                preferred_element_type=jnp.float32,
            )
            / total_rows
        )
        gram = lax.psum(gram, "rows")
        lower = jnp.linalg.cholesky(gram)
        vector = jax.scipy.linalg.solve_triangular(lower, smoothed, lower=True)
    return vector


def solution(mesh):
    in_specs = (
        P("rows", None),
        P("rows"),
        P("rows", "cols", None),
        P("rows", "cols", None),
        P("rows", "cols"),
        P(None, "rows"),
    )
    out_specs = P(None, "rows")
    return jax.shard_map(local, mesh=mesh, in_specs=in_specs, out_specs=out_specs, check_vma=False)
```

profile of v0, /device:TPU:1, one launch (start us, length us, event | category | flops | bytes accessed | tf_op | source)
XLA Modules:
  0.0 1607.4 jit_solution(10756522774581619305)
XLA Ops:
  6.5 2.1 fusion.16
  8.7 2.1 fusion.18
  10.8 4.6 collective-permute-start.2
  15.4 6.8 collective-permute-start.3
  22.3 1.9 collective-permute-start.4
  24.2 1.9 collective-permute-start
  26.1 2.4 collective-permute-start.1
  28.6 9.8 collective-permute-done.4
  38.4 1.9 collective-permute-start.5
  41.5 2.7 collective-permute-done.5
  45.0 5.4 pad_maximum_fusion
  50.8 91.8 %while.24 = (s32[]{:T(128)}, f32[64,1024]{1,0:T(8,128)S(1)}, f32[1,1024]{1,0:T(1,128)S(1)}, bf16[24,256,256]{1,2,0:T(8,128)(2,1)S(1)}, s32[]{:T(128)}, /*index=5...) while((s32[]{:T(128)}, f32[64,1024]{1,0:T(8,128)S(1)}, ...), condition=%wide.region_3.4_spmd, body=%wide.region_1.3_spmd.sunk | while | flops 143213584 | bytes 1750485 | solution.py:110
  59.1 1.6 convert_reduce_fusion.2
  70.5 1.6 convert_reduce_fusion.2
  81.9 1.6 convert_reduce_fusion.2
  93.3 1.6 convert_reduce_fusion.2
  104.7 1.6 convert_reduce_fusion.2
  116.1 1.6 convert_reduce_fusion.2
  127.4 1.6 convert_reduce_fusion.2
  143.4 188.7 %psum.39 = f32[1024]{0:T(1024)S(1)} all-reduce(f32[1024]{0:T(1024)S(1)} %bitcast.61), channel_id=1, replica_groups=mesh['rows'=128,'cols'=4] {'cols'}, use_global_device_ids=true, to_apply=%region_5.6 | all-reduce | flops 1024 | bytes 8192 | tf_op jit(solution)/shard_map/psum | solution.py:111
  332.0 54.4 %all-reduce.3.cloned.1.call-done = f32[64,1024]{1,0:T(8,128)} async-done(((f32[64,1024]{1,0:T(8,128)}), f32[64,1024]{1,0:T(8,128)}) %all-reduce.3.cloned.1.call-update) | async-done | bytes 262160 | tf_op jit(solution)/shard_map/psum | solution.py:111
  387.8 491.5 %psum.40 = f32[64,64]{0,1:T(8,128)S(1)} all-reduce(f32[64,64]{0,1:T(8,128)S(1)} %convolution_multiply_fusion.2), channel_id=1, replica_groups=mesh['rows'=128,'cols'=4] {'rows'}, use_global_device_ids=true, to_apply=%region_6.7 | all-reduce | flops 4096 | bytes 32768 | tf_op jit(solution)/shard_map/psum | solution.py:122
  879.4 5.8 cholesky.44
  886.6 4.9 custom-call.6
  892.9 3.6 collective-permute-start.6
  896.5 5.2 collective-permute-start.7
  903.6 43.7 %while.25 = (s32[]{:T(128)}, f32[64,1024]{1,0:T(8,128)S(1)}, s32[]{:T(128)}, s32[24]{0:T(128)}, s32[24]{0:T(128)}, /*index=5*/bf16[64,3072]{1,0:T(8,128)(2,1)}, ...) while((s32[]{:T(128)}, f32[64,1024]{1,0:T(8,128)S(1)}, ...), condition=%wide.region_10.13_spmd, body=%wide.region_9.12_spmd.sunk | while | flops 8405005 | bytes 295199 | solution.py:110
  948.1 145.3 %all-reduce.5.cloned.1.call-done = f32[64,1024]{1,0:T(8,128)} async-done(((f32[64,1024]{1,0:T(8,128)}), f32[64,1024]{1,0:T(8,128)}) %all-reduce.5.cloned.1.call-update) | async-done | bytes 262160 | tf_op jit(solution)/shard_map/psum | solution.py:111
  1094.7 491.5 %psum.42 = f32[64,64]{0,1:T(8,128)S(1)} all-reduce(f32[64,64]{0,1:T(8,128)S(1)} %convolution_multiply_fusion.1), channel_id=1, replica_groups=mesh['rows'=128,'cols'=4] {'rows'}, use_global_device_ids=true, to_apply=%region_12.15 | all-reduce | flops 4096 | bytes 32768 | tf_op jit(solution)/shard_map/psum | solution.py:122
  1586.4 5.8 cholesky.55
  1593.5 4.9 custom-call.7
  1598.4 2.1 fusion.19
  (138 shorter events, 90.0 us)
Async XLA Ops:
  6.5 15.7 copy-start.3
  6.5 17.6 %copy-start.2 = (f32[64,1024]{1,0:T(8,128)S(1)}, f32[64,1024]{1,0:T(8,128)}, u32[]{:S(2)}) copy-start(f32[64,1024]{1,0:T(8,128)} %param.18) | copy-start | bytes 786436
  6.5 379.9 %all-reduce.3.cloned.1.call-start = ((), (), s32[]{:S(2)}) async-start(), calls=%async_computation | async-start | bytes 524288 | tf_op jit(solution)/shard_map/psum | solution.py:111
  10.8 34.2 %collective-permute-start.2 = (bf16[1024,1024]{1,0:T(8,128)(2,1)S(1)}, bf16[1024,1024]{1,0:T(8,128)(2,1)}, u32[]{:S(2)}, u32[]{:S(2)}) collective-permute-start(bf16[1024,1024]{1,0:T(8,128)(2,1)S(1)} %fusion.18), channel_id=1, source_target_pairs={{0,4},{4,8},{8,12},{12,16},{16,20},{20,24},{24,28},{28,32},{32,36}... | collective-permute-start | bytes 6291464 | tf_op jit(solution)/shard_map/ppermute | solution.py:25
  15.4 29.6 %collective-permute-start.3 = (bf16[1024,1024]{1,0:T(8,128)(2,1)S(1)}, bf16[1024,1024]{1,0:T(8,128)(2,1)}, u32[]{:S(2)}, u32[]{:S(2)}) collective-permute-start(bf16[1024,1024]{1,0:T(8,128)(2,1)S(1)} %fusion.18), channel_id=1, source_target_pairs={{4,0},{8,4},{12,8},{16,12},{20,16},{24,20},{28,24},{32,28},{36,32}... | collective-permute-start | bytes 6291464 | tf_op jit(solution)/shard_map/ppermute | solution.py:27
  22.3 16.1 %collective-permute-start.4 = (bf16[1024]{0:T(1024)(128)(2,1)S(1)}, bf16[1024]{0:T(1024)(128)(2,1)S(1)}, u32[]{:S(2)}, u32[]{:S(2)}) collective-permute-start(bf16[1024]{0:T(1024)(128)(2,1)S(1)} %copy-done.3), channel_id=1, source_target_pairs={{0,4},{4,8},{8,12},{12,16},{16,20},{20,24},{24,28},{28,32},{32,36}... | collective-permute-start | bytes 6152 | tf_op jit(solution)/shard_map/ppermute | solution.py:25
  24.2 20.0 %collective-permute-start = (bf16[64,1024]{1,0:T(8,128)(2,1)S(1)}, bf16[64,1024]{1,0:T(8,128)(2,1)S(1)}, u32[]{:S(2)}, u32[]{:S(2)}) collective-permute-start(bf16[64,1024]{1,0:T(8,128)(2,1)S(1)} %convert_element_type.24), channel_id=1, source_target_pairs={{0,4},{4,8},{8,12},{12,16},{16,20},{20,24},{24,28},{28,32},{32,36}... | collective-permute-start | bytes 393224 | tf_op jit(solution)/shard_map/ppermute | solution.py:25
  26.1 18.0 %collective-permute-start.1 = (bf16[64,1024]{1,0:T(8,128)(2,1)S(1)}, bf16[64,1024]{1,0:T(8,128)(2,1)S(1)}, u32[]{:S(2)}, u32[]{:S(2)}) collective-permute-start(bf16[64,1024]{1,0:T(8,128)(2,1)S(1)} %convert_element_type.24), channel_id=1, source_target_pairs={{4,0},{8,4},{12,8},{16,12},{20,16},{24,20},{28,24},{32,28},{36,32}... | collective-permute-start | bytes 393224 | tf_op jit(solution)/shard_map/ppermute | solution.py:27
  38.4 5.8 collective-permute-start.5
  142.6 0.7 copy-start
  143.3 950.0 %all-reduce.5.cloned.1.call-start = ((), (), s32[]{:S(2)}) async-start(), calls=%async_computation.1 | async-start | bytes 524288 | tf_op jit(solution)/shard_map/psum | solution.py:111
  892.9 8.9 collective-permute-start.6
  896.5 6.3 collective-permute-start.7
  947.3 0.7 copy-start.1
Sparse Core Ops, SparseCore 0:
  143.4 242.9 all-reduce.2
  948.2 145.0 all-reduce.4
where the time goes:
time: 1620 us; the launch traced here: 1610 us
  blocking collectives  1170 us (72%)
  waiting for transfers between devices  213 us (13%)
  local copies, waits for them, and re-layouts  62.3 us (4%)
  loops' own time  47.1 us (3%)
  other arithmetic  37.5 us (2%)
  matrix products  33.4 us (2%)
  starting transfers between devices  28.5 us (2%)
    psum x2, blocking collectives, local(): gram = lax.psum(gram, 'rows')  983 us
    psum x2, waiting for transfers between devices, local(): summed, degree = lax.psum((partial_value, degree_part), 'cols')  200 us
    psum x1, blocking collectives, local(): summed, degree = lax.psum((partial_value, degree_part), 'cols')  189 us
    another operation x2, loops' own time, local(): lax.fori_loop(0, live_count, accumulate, start_state)  47.1 us
  transfers between devices with their start and end apart: 10, of which 5 were waited for; matrix products, arithmetic and copies ran while one was open for 0% of the time, Pallas kernels for 0%

commit v1 on v0

v1 whole, which is shorter than its diff:
```python
import functools

import jax
import jax.numpy as jnp
from jax import lax
from jax.experimental import pallas as pl
from jax.experimental.pallas import tpu as pltpu
from jax.sharding import PartitionSpec as P

MESH = pl.DeviceIdType.MESH
NY, NC = 4, 2
K = 64
KA = 80
KD = 72
sharpness = 10.0
epsilon = 1e-06

F32 = jnp.float32
BF16 = jnp.bfloat16
HIGH = lax.Precision.HIGHEST


def dot_nt(a, b, precision=None):
    return lax.dot_general(
        a, b, (((1,), (1,)), ((), ())), precision=precision, preferred_element_type=F32
    )


def dot_nn(a, b, precision=None):
    return jnp.dot(a, b, precision=precision, preferred_element_type=F32)


def normalize(src, dst, rows):
    width = src.shape[1]
    chunk = 32

    def body(c, carry):
        at = pl.ds(pl.multiple_of(c * chunk, chunk), chunk)
        values = src[at, :].astype(F32)
        square = jnp.sum(values * values, axis=1, keepdims=True) * (1.0 / width)
        scale = lax.rsqrt(square + epsilon) * (1.0 / width**0.5)
        dst[at, :] = (values * scale).astype(BF16)
        return carry

    lax.fori_loop(0, rows // chunk, body, 0)


def inverse_factor(matrix):
    lane = lax.broadcasted_iota(jnp.int32, (8, 2 * K), 1)
    row8 = lax.broadcasted_iota(jnp.int32, (8, 2 * K), 0)
    work = [
        jnp.where(lane < K, matrix[8 * m : 8 * m + 8, :], (lane - K == row8 + 8 * m).astype(F32))
        for m in range(K // 8)
    ]
    pivots = [None] * (K // 8)
    for k in range(K):
        m0, s = k // 8, k % 8
        row = jnp.broadcast_to(work[m0][s : s + 1, :], (8, 2 * K))
        pivot = jnp.broadcast_to(row[:, k : k + 1], (8, 2 * K))
        ratio = row / pivot
        here = row8 == s
        pivots[m0] = pivot if pivots[m0] is None else jnp.where(here, pivot, pivots[m0])
        for m in range(m0, K // 8):
            column = jnp.broadcast_to(work[m][:, k : k + 1], (8, 2 * K))
            update = column * ratio
            if m == m0:
                if s == 7:
                    continue
                update = jnp.where(row8 > s, update, 0.0)
            work[m] = work[m] - update
    done = [work[m] * lax.rsqrt(pivots[m]) for m in range(K // 8)]
    return jnp.concatenate(done, axis=0)[:, K:]


def kernel(
    nz, ny, nc, nx, total_rows,
    emb, knn, prow, pcol, pcnt, start,
    out,
    emb_v, unit, emb_h, unit_h, km, km_h, mcol, v0, v0_h, sc, aff, part1, part2, rs1, rs2,
    nar, nar_h, mask, mask_x, msum, yall, gpart, ga, gsum, gb, gsum2, gc, gfull,
    local_sem, emb_s, emb_r, km_s, km_r, v0_s, v0_r, mask_s, mask_r,
    rs1_s, rs1_r, rs2_s, rs2_r, nar_s, nar_r, y_s, y_r,
    ga_s, ga_r, gb_s, gb_r, gc_s, gc_r, gd_s, gd_r,
):
    g = lax.axis_index("rows")
    x = lax.axis_index("cols")
    rows = nz * ny * nc
    core = g % nc
    y = (g // nc) % ny
    z = g // (nc * ny)
    block = emb_h.shape[1]
    here = emb_v.shape[0]
    blocks = here // block
    parts = nc * nx

    def at(dz=0, dy=0, dc=0, dx=0):
        row = (((z + dz) % nz) * ny + (y + dy) % ny) * nc + (core + dc) % nc
        return (row, (x + dx) % nx)

    sides = [((g + 1) % rows, x), ((g + rows - 1) % rows, x)]
    near = [(e // nx, e % nx) for e in range(1, parts)]
    xpeers = [at(dx=d) for d in range(1, nx)]
    npeers = [at(dc=dc, dx=dx) for dc, dx in near]
    ypeers = [at(dy=d) for d in range(1, ny)]
    zpeers = [at(dz=d) for d in range(1, nz)]

    barrier = pltpu.get_barrier_semaphore()
    everyone = sides + npeers + ypeers + zpeers
    for peer in everyone:
        pl.semaphore_signal(barrier, inc=1, device_id=peer, device_id_type=MESH)

    started = []

    def remote(src, dst, ssem, rsem, peer):
        return pltpu.make_async_remote_copy(
            src_ref=src, dst_ref=dst, send_sem=ssem, recv_sem=rsem,
            device_id=peer, device_id_type=MESH,
        )

    def send(src, dst, ssem, rsem, peer):
        copy = remote(src, dst, ssem, rsem, peer)
        copy.start()
        started.append(copy)
        return copy

    own = pl.ds(pl.multiple_of(x * block, block), block)
    for r in range(blocks):
        pltpu.make_async_copy(
            emb.at[pl.ds(r * block, block)], emb_v.at[pl.ds(r * block, block)], local_sem.at[r]
        ).start()
    load_v = pltpu.make_async_copy(start.at[:, own], v0, local_sem.at[blocks])
    load_v.start()

    slots = prow.shape[-1]
    spot = (prow[0] - g * blocks) * (3 * blocks) + (pcol[0] - (g - 1) * blocks)
    live = lax.broadcasted_iota(jnp.int32, (1, slots), 1) < pcnt[...]
    spot = jnp.where(live, spot, -1)
    hit = lax.broadcasted_iota(jnp.int32, (mask.shape[0], slots), 0) == spot
    mask[...] = jnp.broadcast_to(
        jnp.sum(jnp.where(hit, 1.0, 0.0), axis=1, keepdims=True), mask.shape
    )
    means = knn[...].astype(F32)
    for r in range(blocks):
        km[r] = jnp.broadcast_to(means[:, r * block : (r + 1) * block], (8, block))

    pl.semaphore_wait(barrier, len(everyone))

    for h, peer in enumerate(sides):
        send(km.at[x], km_h.at[h], km_s.at[h], km_r.at[h], peer)
    for h, peer in enumerate(sides):
        send(start.at[:, own], v0_h.at[h], v0_s.at[h], v0_r.at[h], peer)
    for h, peer in enumerate(sides):
        send(emb.at[own], emb_h.at[h], emb_s.at[h], emb_r.at[h], peer)
    masks = [
        send(mask, mask_x.at[d], mask_s.at[d], mask_r.at[d], peer) for d, peer in enumerate(xpeers)
    ]

    for r in range(blocks):
        where = pl.ds(r * block, block)
        pltpu.make_async_copy(emb.at[where], emb_v.at[where], local_sem.at[r]).wait()
        normalize(emb_v.at[where], unit.at[where], block)
    lane = lax.broadcasted_iota(jnp.int32, (block, block), 1)
    line = lax.broadcasted_iota(jnp.int32, (block, block), 0)
    eye = jnp.where(lane == line, 1.0, 0.0).astype(BF16)
    for r in range(blocks):
        wide = jnp.broadcast_to(km[r, 0:1, :], (128, block)).astype(BF16)
        mcol[pl.ds(r * block, block), :] = dot_nt(eye, wide)

    chunk = 64

    def affinity(slot, unit_col, mean_row, diagonal):
        sc[...] = dot_nt(unit[...], unit_col)

        def body(c, carry):
            rows_at = pl.ds(pl.multiple_of(c * chunk, chunk), chunk)
            side = mcol[rows_at, :]
            denom = 0.5 * (jnp.concatenate([side] * (block // 128), axis=1) + mean_row)
            weights = jnp.exp(sharpness * sc[rows_at, :] / denom)
            if diagonal:
                a = lax.broadcasted_iota(jnp.int32, (chunk, block), 0) + c * chunk
                b = lax.broadcasted_iota(jnp.int32, (chunk, block), 1) + x * block
                weights = jnp.where(a == b, 0.0, weights)
            aff[slot, rows_at, :] = weights.astype(BF16)
            return carry

        lax.fori_loop(0, here // chunk, body, 0)

    def product(slot, window, source, part, first):
        for r in range(blocks):
            live_pair = msum[pl.ds(r * 3 * blocks + window * blocks + x, 1), :][:, 0:1]
            piece = dot_nt(source, aff[slot, pl.ds(r * block, block), :]) * live_pair
            part[r, pl.ds(0, piece.shape[0]), :] = (
                piece if first else part[r, pl.ds(0, piece.shape[0]), :] + piece
            )

    tail = lax.broadcasted_iota(jnp.int32, (KA - K, block), 0)
    ones = jnp.where(tail == 0, 1.0, 0.0)

    def widened(values):
        return jnp.concatenate([values, ones], axis=0).astype(BF16)

    affinity(2, unit[own, :], km[x, 0:1, :], True)
    for c in masks:
        c.wait_recv()
    msum[...] = mask[...]
    for d in range(nx - 1):
        msum[...] += mask_x[d]
    load_v.wait()
    product(2, 1, widened(v0[...]), part1, True)

    def side(step, carry):
        h = (core + 1 + step) % 2
        remote(km.at[x], km_h.at[h], km_s.at[h], km_r.at[h], sides[0]).wait_recv()
        remote(start.at[:, own], v0_h.at[h], v0_s.at[h], v0_r.at[h], sides[0]).wait_recv()
        remote(emb.at[own], emb_h.at[h], emb_s.at[h], emb_r.at[h], sides[0]).wait_recv()
        normalize(emb_h.at[h], unit_h, block)
        affinity(h, unit_h[...], km_h[h, 0:1, :], False)
        product(h, 2 * h, widened(v0_h[h]), part1, False)
        return carry

    lax.fori_loop(0, 2, side, 0)

    scatter = [
        send(part1.at[(x + d) % nx, pl.ds(0, KD)], rs1.at[d - 1], rs1_s.at[d - 1], rs1_r.at[d - 1], peer)
        for d, peer in zip(range(1, nx), xpeers)
    ]
    for c in scatter:
        c.wait_recv()
    total = part1[x, pl.ds(0, KD), :]
    for d in range(nx - 1):
        total = total + rs1[d]
    degree = total[K : K + 1, :]
    smoothed1 = total[:K, :] / degree
    nar[...] = smoothed1.astype(BF16)

    narrow = [send(nar, nar_h.at[h], nar_s.at[h], nar_r.at[h], peer) for h, peer in enumerate(sides)]
    gram1 = dot_nt(smoothed1, smoothed1, HIGH) * (1.0 / total_rows)
    product(2, 1, nar[...], part2, True)
    for c in narrow:
        c.wait_recv()
    for h in range(2):
        product(h, 2 * h, nar_h[h], part2, False)
    scatter = [
        send(part2.at[(x + d) % nx], rs2.at[d - 1], rs2_s.at[d - 1], rs2_r.at[d - 1], peer)
        for d, peer in zip(range(1, nx), xpeers)
    ]
    for c in scatter:
        c.wait_recv()
    total = part2[x]
    for d in range(nx - 1):
        total = total + rs2[d]
    smoothed2 = total / degree
    yall[0] = smoothed2
    gather = [
        send(yall.at[0], yall.at[d], y_s.at[d - 1], y_r.at[d - 1], peer)
        for d, peer in zip(range(1, nx), xpeers)
    ]

    gram2 = dot_nt(smoothed2, smoothed2, HIGH) * (1.0 / total_rows)
    both = jnp.concatenate([gram1, gram2], axis=1)
    height = K // parts
    for p in range(parts):
        gpart[p] = both[p * height : (p + 1) * height, :]
    copies = [
        send(
            gpart.at[((core + dc) % nc) * nx + (x + dx) % nx], ga.at[e], ga_s.at[e], ga_r.at[e], peer
        )
        for e, ((dc, dx), peer) in enumerate(zip(near, npeers))
    ]
    for c in copies:
        c.wait_recv()
    total = gpart[core * nx + x]
    for e in range(parts - 1):
        total = total + ga[e]
    gsum[...] = total
    copies = [
        send(gsum, gb.at[d], gb_s.at[d], gb_r.at[d], peer) for d, peer in enumerate(ypeers)
    ]
    for c in copies:
        c.wait_recv()
    for d in range(ny - 1):
        total = total + gb[d]
    gsum2[...] = total
    copies = [
        send(gsum2, gc.at[d], gc_s.at[d], gc_r.at[d], peer) for d, peer in enumerate(zpeers)
    ]
    for c in copies:
        c.wait_recv()
    for d in range(nz - 1):
        total = total + gc[d]
    gfull[0] = total
    copies = [
        send(gfull.at[0], gfull.at[e + 1], gd_s.at[e], gd_r.at[e], peer)
        for e, peer in enumerate(npeers)
    ]
    for c in copies:
        c.wait_recv()
    gram = jnp.concatenate(
        [gfull[((core + nc - p // nx) % nc) * nx + (x + nx - p % nx) % nx] for p in range(parts)],
        axis=0,
    )

    first = inverse_factor(gram)
    inner = dot_nt(dot_nn(first, gram[:, K:], HIGH), first, HIGH)
    second = inverse_factor(jnp.concatenate([inner, inner], axis=1))
    whiten = dot_nn(second, first, HIGH)
    for c in gather:
        c.wait_recv()
    for p in range(nx):
        out[:, pl.ds(p * block, block)] = dot_nn(whiten, yall[(x + nx - p) % nx], HIGH)
    for c in started:
        c.wait_send()


def solution(mesh):
    nx = mesh.shape["cols"]
    groups = mesh.shape["rows"]
    nz = groups // (NY * NC)
    parts = NC * nx

    def local(embeddings, knn_mean, pair_rows, pair_cols, pair_count, start_block):
        here, width = embeddings.shape
        block = here // nx
        height = K // parts
        dma = pltpu.SemaphoreType.DMA
        vmem = pl.BlockSpec(memory_space=pltpu.VMEM)
        hbm = pl.BlockSpec(memory_space=pl.ANY)
        return pl.pallas_call(
            functools.partial(kernel, nz, NY, NC, nx, here * groups),
            out_shape=jax.ShapeDtypeStruct((K, here), F32),
            in_specs=[hbm, vmem, vmem, vmem, vmem, hbm],
            out_specs=vmem,
            scratch_shapes=[
                pltpu.VMEM((here, width), BF16),
                pltpu.VMEM((here, width), BF16),
                pltpu.VMEM((2, block, width), BF16),
                pltpu.VMEM((block, width), BF16),
                pltpu.VMEM((nx, 8, block), F32),
                pltpu.VMEM((2, 8, block), F32),
                pltpu.VMEM((here, 128), F32),
                pltpu.VMEM((K, block), F32),
                pltpu.VMEM((2, K, block), F32),
                pltpu.VMEM((here, block), F32),
                pltpu.VMEM((3, here, block), BF16),
                pltpu.VMEM((nx, KA, block), F32),
                pltpu.VMEM((nx, K, block), F32),
                pltpu.VMEM((nx - 1, KD, block), F32),
                pltpu.VMEM((nx - 1, K, block), F32),
                pltpu.VMEM((K, block), BF16),
                pltpu.VMEM((2, K, block), BF16),
                pltpu.VMEM((3 * nx * nx, 128), F32),
                pltpu.VMEM((nx - 1, 3 * nx * nx, 128), F32),
                pltpu.VMEM((3 * nx * nx, 128), F32),
                pltpu.VMEM((nx, K, block), F32),
                pltpu.VMEM((parts, height, 2 * K), F32),
                pltpu.VMEM((parts - 1, height, 2 * K), F32),
                pltpu.VMEM((height, 2 * K), F32),
                pltpu.VMEM((NY - 1, height, 2 * K), F32),
                pltpu.VMEM((height, 2 * K), F32),
                pltpu.VMEM((nz - 1, height, 2 * K), F32),
                pltpu.VMEM((parts, height, 2 * K), F32),
                dma((nx + 1,)),
                dma((2,)), dma((2,)), dma((2,)), dma((2,)), dma((2,)), dma((2,)),
                dma((nx - 1,)), dma((nx - 1,)),
                dma((nx - 1,)), dma((nx - 1,)),
                dma((nx - 1,)), dma((nx - 1,)),
                dma((2,)), dma((2,)),
                dma((nx - 1,)), dma((nx - 1,)),
                dma((parts - 1,)), dma((parts - 1,)),
                dma((NY - 1,)), dma((NY - 1,)),
                dma((nz - 1,)), dma((nz - 1,)),
                dma((parts - 1,)), dma((parts - 1,)),
            ],
            compiler_params=pltpu.CompilerParams(collective_id=0, has_side_effects=True),
        )(embeddings, knn_mean.reshape(1, here), pair_rows, pair_cols, pair_count, start_block)

    in_specs = (
        P("rows", None),
        P("rows"),
        P("rows", "cols", None),
        P("rows", "cols", None),
        P("rows", "cols"),
        P(None, "rows"),
    )
    out_specs = P(None, "rows")
    return jax.shard_map(local, mesh=mesh, in_specs=in_specs, out_specs=out_specs, check_vma=False)
```

time: 1620 us -> 85.2 us (0.05)
  blocking collectives: 1170 us -> 0 us
  waiting for transfers between devices: 213 us -> 0 us
  Pallas kernels: 0 us -> 81.4 us
  local copies, waits for them, and re-layouts: 62.3 us -> 2.95 us
  loops' own time: 47.1 us -> 0 us
  other arithmetic: 37.5 us -> 0 us
  matrix products: 33.4 us -> 0 us
  starting transfers between devices: 28.5 us -> 0 us
    psum x3 -> x0, blocking collectives: 1170 us -> none  [the longest x2 983 us: local(): gram = lax.psum(gram, 'rows')]
    psum x2 -> x0, waiting for transfers between devices: 200 us -> none  [local(): summed, degree = lax.psum((partial_value, degree_part), 'cols')]
    pallas_call x0 -> x1, Pallas kernels: none -> 81.4 us  [local(): pl.pallas_call(functools.partial(kernel, nz, NY, NC, nx, here * groups),...]
    dynamic_slice x48 -> x0, local copies, waits for them, and re-layouts: 60.2 us -> none  [the longest x16 19.8 us: accumulate(): row_block = local_rows[slot]]
    another operation x2 -> x0, loops' own time: 47.1 us -> none  [local(): lax.fori_loop(0, live_count, accumulate, start_state)]
    dot_general x26 -> x0, matrix products: 29.9 us -> none  [the longest x16 14.5 us: accumulate(): lax.dot_general(source, affinity, (((1,), (1,)), ((), ())), preferred_ele...]
    ppermute x8 -> x0, starting transfers between devices: 28.4 us -> none  [the longest x4 16.4 us: extended(): lax.ppermute(head, axis, [((i + 1) % count, i) for i in range(ends)])]
    another operation x10 -> x0, other arithmetic: 24.1 us -> none  [the longest x6 13 us: local(): lower = jnp.linalg.cholesky(gram)]
  transfers between devices with their start and end apart: 10 -> 0, of which waited for: 5 -> 0; matrix products, arithmetic and copies ran while one was open for 0% -> 0% of each run, Pallas kernels for 0% -> 0%
where the time goes in v1:
time: 85.2 us; the launch traced here: 85 us
  Pallas kernels  81.4 us (96%)
  local copies, waits for them, and re-layouts  2.95 us (3%)
    pallas_call x1, Pallas kernels, local(): pl.pallas_call(functools.partial(kernel, nz, NY, NC, nx, here * groups),...  81.4 us

profile of v1, /device:TPU:1, one launch (start us, length us, event | category | flops | bytes accessed | tf_op | source)
XLA Modules:
  0.0 85.0 jit_solution(10276547885409891594)
XLA Ops:
  0.7 1.3 %reshape.3.knn = bf16[1,1024]{1,0:T(2,128)(2,1)} reshape(bf16[1024]{0:T(1024)(128)(2,1)} %param.7) | data formatting | bytes 4096 | tf_op jit(solution)/shard_map/reshape | solution.py:375
  1.9 81.4 %shard_map.64 = f32[64,1024]{1,0:T(8,128)} custom-call(bf16[1024,1024]{1,0:T(8,128)(2,1)} %emb.1, bf16[1,1024]{1,0:T(2,128)(2,1)} %reshape.3.knn, s32[1,1,24]{2,1,0:T(1,128)} %prow.1, s32[1,1,24]{2,1,0:T(1,128)} %pcol.1, s32[1,1]{1,0:T(1,128)S(6)} %copy.8.pcnt, f32[64,1024]{1,0:T(8,128)} %start.1), custom_call_target="tpu_custom_call" | custom-call | tf_op jit(solution)/shard_map/pallas_call | solution.py:328
  83.3 1.7 %copy.9 = f32[64,1024]{1,0:T(8,128)} copy(f32[64,1024]{1,0:T(8,128)} %shard_map.64) | data formatting | bytes 524288

commit v2 on v1

v2 whole, which is shorter than its diff:
```python
import functools

import jax
import jax.numpy as jnp
from jax import lax
from jax.experimental import pallas as pl
from jax.experimental.pallas import tpu as pltpu
from jax.sharding import PartitionSpec as P

MESH = pl.DeviceIdType.MESH
NY, NC = 4, 2
K = 64
KA = 80
KD = 72
PANEL = 8
sharpness = 10.0
epsilon = 1e-06

F32 = jnp.float32
BF16 = jnp.bfloat16
HIGH = lax.Precision.HIGHEST


def dot_nt(a, b, precision=None):
    return lax.dot_general(
        a, b, (((1,), (1,)), ((), ())), precision=precision, preferred_element_type=F32
    )


def dot_nn(a, b, precision=None):
    return jnp.dot(a, b, precision=precision, preferred_element_type=F32)


def normalize(src, dst, rows):
    width = src.shape[1]
    chunk = 64

    def body(c, carry):
        at = pl.ds(pl.multiple_of(c * chunk, chunk), chunk)
        values = src[at, :].astype(F32)
        square = jnp.sum(values * values, axis=1, keepdims=True) * (1.0 / width)
        scale = lax.rsqrt(square + epsilon) * (1.0 / width**0.5)
        dst[at, :] = (values * scale).astype(BF16)
        return carry

    lax.fori_loop(0, rows // chunk, body, 0, unroll=4)


def inverse_factor(matrix):
    wide = (8, 2 * K)
    lane = lax.broadcasted_iota(jnp.int32, wide, 1)
    row8 = lax.broadcasted_iota(jnp.int32, wide, 0)
    tall = K // 8

    def spread(values, k):
        return jnp.broadcast_to(values[:, k : k + 1], wide)

    blocks = [matrix[8 * m : 8 * m + 8, :] for m in range(tall)]
    marks = [lane == row8 + 8 * m for m in range(tall)]
    diagonals = [jnp.where(marks[m], blocks[m], 0.0) for m in range(tall)]
    along = sum(diagonals[1:], diagonals[0])
    along = jnp.broadcast_to(jnp.sum(along, axis=0, keepdims=True), wide)
    along = lax.rsqrt(jnp.where(lane < K, along, 1.0))
    work = []
    for m in range(tall):
        down = lax.rsqrt(jnp.broadcast_to(jnp.sum(diagonals[m], axis=1, keepdims=True), wide))
        right = jnp.where(lane - K == row8 + 8 * m, down, 0.0)
        work.append(jnp.where(lane < K, blocks[m] * down * along, right))
    done = []
    for m0 in range(tall):
        k = m0 * PANEL
        rows = [jnp.broadcast_to(work[m0][t : t + 1, :], wide) for t in range(PANEL)]
        a = {(t, u): spread(rows[t], k + u) for t in range(PANEL) for u in range(t, PANEL)}
        low, inv, pivot = {}, [None] * PANEL, [None] * PANEL
        for t in range(0, PANEL, 2):
            p, q = a[t, t], a[t, t + 1]
            det = p * a[t + 1, t + 1] - q * q
            inv[t] = 1.0 / p
            inv[t + 1] = p * (1.0 / det)
            pivot[t], pivot[t + 1] = p, det * inv[t]
            low[t + 1, t] = q * inv[t]
            for u in range(t + 2, PANEL):
                low[u, t] = a[t, u] * inv[t]
                a[t + 1, u] = a[t + 1, u] - low[t + 1, t] * a[t, u]
                low[u, t + 1] = a[t + 1, u] * inv[t + 1]
            for u in range(t + 2, PANEL):
                for v in range(u, PANEL):
                    a[u, v] = a[u, v] - low[u, t] * a[t, v] - low[u, t + 1] * a[t + 1, v]
        for t in range(1, PANEL):
            for u in range(t):
                rows[t] = rows[t] - low[t, u] * rows[u]
        scaled = [rows[t] * inv[t] for t in range(PANEL)]
        for m in range(m0 + 1, tall):
            column = [spread(work[m], k + t) for t in range(PANEL)]
            for t in range(1, PANEL):
                for u in range(t):
                    column[t] = column[t] - low[t, u] * column[u]
            for t in range(PANEL):
                work[m] = work[m] - column[t] * scaled[t]
        reduced, pivots = rows[0], pivot[0]
        for t in range(1, PANEL):
            reduced = jnp.where(row8 == t, rows[t], reduced)
            pivots = jnp.where(row8 == t, pivot[t], pivots)
        done.append(reduced * lax.rsqrt(pivots))
    return jnp.concatenate(done, axis=0)[:, K:]


def kernel(
    nz, ny, nc, nx, total_rows,
    emb, knn, prow, pcol, pcnt, start,
    out,
    emb_v, unit, emb_h, unit_h, km, km_h, mcol, v0, v0_h, aff, part1, half1, part2, rs1, rs1_d, rs2,
    nar, nar_h, mask, mask_x, msum, yall, gpart, ga, gsum, gb, gsum2, gc, gfull,
    local_sem, emb_s, emb_r, km_s, km_r, v0_s, v0_r, mask_s, mask_r,
    rs1_s, rs1_r, rsd_s, rsd_r, rs2_s, rs2_r, nar_s, nar_r, y_s, y_r,
    ga_s, ga_r, gb_s, gb_r, gc_s, gc_r, gd_s, gd_r, reach_sem,
):
    g = lax.axis_index("rows")
    x = lax.axis_index("cols")
    rows = nz * ny * nc
    core = g % nc
    y = (g // nc) % ny
    z = g // (nc * ny)
    block = emb_h.shape[1]
    here = emb_v.shape[0]
    blocks = here // block
    parts = nc * nx

    def at(dz=0, dy=0, dc=0, dx=0):
        row = (((z + dz) % nz) * ny + (y + dy) % ny) * nc + (core + dc) % nc
        return (row, (x + dx) % nx)

    sides = [((g + 1) % rows, x), ((g + rows - 1) % rows, x)]
    near = [(e // nx, e % nx) for e in range(1, parts)]
    xpeers = [at(dx=d) for d in range(1, nx)]
    npeers = [at(dc=dc, dx=dx) for dc, dx in near]
    ypeers = [at(dy=d) for d in range(1, ny)]
    zpeers = [at(dz=d) for d in range(1, nz)]

    barrier = pltpu.get_barrier_semaphore()
    zreach = [d for d in range(1, nz) if min(d, nz - d) <= 2]
    rounds = []
    while 2 * 2 ** len(rounds) < nz // 2:
        rounds.append(2 * 2 ** len(rounds))
    everyone = sides + npeers + ypeers + [at(dz=d) for d in zreach]
    for peer in everyone:
        pl.semaphore_signal(barrier, inc=1, device_id=peer, device_id_type=MESH)

    started = []

    def remote(src, dst, ssem, rsem, peer):
        return pltpu.make_async_remote_copy(
            src_ref=src, dst_ref=dst, send_sem=ssem, recv_sem=rsem,
            device_id=peer, device_id_type=MESH,
        )

    def send(src, dst, ssem, rsem, peer):
        copy = remote(src, dst, ssem, rsem, peer)
        copy.start()
        started.append(copy)
        return copy

    own = pl.ds(pl.multiple_of(x * block, block), block)
    for r in range(blocks):
        pltpu.make_async_copy(
            emb.at[pl.ds(r * block, block)], emb_v.at[pl.ds(r * block, block)], local_sem.at[r]
        ).start()
    load_v = pltpu.make_async_copy(start.at[:, own], v0, local_sem.at[blocks])
    load_v.start()

    slots = prow.shape[-1]
    spot = (prow[0] - g * blocks) * (3 * blocks) + (pcol[0] - (g - 1) * blocks)
    live = lax.broadcasted_iota(jnp.int32, (1, slots), 1) < pcnt[...]
    spot = jnp.where(live, spot, -1)
    hit = lax.broadcasted_iota(jnp.int32, (mask.shape[0], slots), 0) == spot
    mask[...] = jnp.broadcast_to(
        jnp.sum(jnp.where(hit, 1.0, 0.0), axis=1, keepdims=True), mask.shape
    )
    means = knn[...].astype(F32).reshape(1, here)
    for r in range(blocks):
        km[r] = jnp.broadcast_to(means[:, r * block : (r + 1) * block], (8, block))

    def reach_signal(n):
        for dz in (rounds[n], -rounds[n]):
            pl.semaphore_signal(
                reach_sem.at[n], inc=1, device_id=at(dz=nz + dz), device_id_type=MESH
            )

    pl.semaphore_wait(barrier, len(everyone))

    for h, peer in enumerate(sides):
        send(km.at[x], km_h.at[h], km_s.at[h], km_r.at[h], peer)
    for h, peer in enumerate(sides):
        send(emb.at[own], emb_h.at[h], emb_s.at[h], emb_r.at[h], peer)
    for h, peer in enumerate(sides):
        send(start.at[:, own], v0_h.at[h], v0_s.at[h], v0_r.at[h], peer)
    masks = [
        send(mask, mask_x.at[d], mask_s.at[d], mask_r.at[d], peer) for d, peer in enumerate(xpeers)
    ]

    if rounds:
        reach_signal(0)

    for r in range(blocks):
        where = pl.ds(r * block, block)
        pltpu.make_async_copy(emb.at[where], emb_v.at[where], local_sem.at[r]).wait()
        normalize(emb_v.at[where], unit.at[where], block)
    lane = lax.broadcasted_iota(jnp.int32, (block, block), 1)
    line = lax.broadcasted_iota(jnp.int32, (block, block), 0)
    eye = jnp.where(lane == line, 1.0, 0.0).astype(BF16)
    for r in range(blocks):
        wide = jnp.broadcast_to(km[r, 0:1, :], (128, block)).astype(BF16)
        mcol[pl.ds(r * block, block), :] = dot_nt(eye, wide)

    def affinity(slot, unit_col, mean_row, diagonal):
        for r in range(blocks):
            rows_at = pl.ds(r * block, block)
            scores = dot_nt(unit[rows_at, :], unit_col)
            side = jnp.concatenate([mcol[rows_at, :]] * (block // 128), axis=1)
            denom = 0.5 * (side + mean_row)
            weights = jnp.exp(sharpness * scores / denom)
            if diagonal:
                weights = jnp.where((lane == line) & (x == r), 0.0, weights)
            aff[slot, rows_at, :] = weights.astype(BF16)

    def product(slot, window, source, part, first):
        for r in range(blocks):
            live_pair = msum[pl.ds(r * 3 * blocks + window * blocks + x, 1), :][:, 0:1]
            piece = dot_nt(source, aff[slot, pl.ds(r * block, block), :]) * live_pair
            part[r, pl.ds(0, piece.shape[0]), :] = (
                piece if first else part[r, pl.ds(0, piece.shape[0]), :] + piece
            )

    tail = lax.broadcasted_iota(jnp.int32, (KA - K, block), 0)
    ones = jnp.where(tail == 0, 1.0, 0.0)

    def widened(values):
        return jnp.concatenate([values, ones], axis=0).astype(BF16)

    affinity(2, unit[own, :], km[x, 0:1, :], True)
    for c in masks:
        c.wait_recv()
    msum[...] = mask[...]
    for d in range(nx - 1):
        msum[...] += mask_x[d]
    load_v.wait()
    product(2, 1, widened(v0[...]), part1, True)

    for n in range(len(rounds)):
        pl.semaphore_wait(reach_sem.at[n], 2)
        if n + 1 < len(rounds):
            reach_signal(n + 1)

    def side(step, carry):
        h = (core + 1 + step) % 2
        remote(km.at[x], km_h.at[h], km_s.at[h], km_r.at[h], sides[0]).wait_recv()
        remote(emb.at[own], emb_h.at[h], emb_s.at[h], emb_r.at[h], sides[0]).wait_recv()
        normalize(emb_h.at[h], unit_h, block)
        affinity(h, unit_h[...], km_h[h, 0:1, :], False)
        remote(start.at[:, own], v0_h.at[h], v0_s.at[h], v0_r.at[h], sides[0]).wait_recv()
        product(h, 2 * h, widened(v0_h[h]), part1, False)
        return carry

    lax.fori_loop(0, 2, side, 0)

    for r in range(blocks):
        half1[r] = part1[r, pl.ds(0, K), :].astype(BF16)
    scatter = []
    for d, peer in zip(range(1, nx), xpeers):
        p, e = (x + d) % nx, d - 1
        scatter.append(send(half1.at[p], rs1.at[e], rs1_s.at[e], rs1_r.at[e], peer))
        scatter.append(
            send(part1.at[p, pl.ds(K, KD - K)], rs1_d.at[e], rsd_s.at[e], rsd_r.at[e], peer)
        )
    for c in scatter:
        c.wait_recv()
    total = part1[x, pl.ds(0, K), :]
    degree = part1[x, pl.ds(K, KD - K), :]
    for d in range(nx - 1):
        total = total + rs1[d].astype(F32)
        degree = degree + rs1_d[d]
    degree = degree[0:1, :]
    smoothed1 = total / degree
    nar[...] = smoothed1.astype(BF16)

    height = K // parts
    me = core * nx + x

    def gram_a(q, smoothed):
        gram = dot_nt(smoothed, smoothed, HIGH) * (1.0 / total_rows)
        gram = jnp.concatenate([gram, jnp.zeros_like(gram)], axis=1)
        for p in range(parts):
            gpart[q, p] = gram[p * height : (p + 1) * height, :]
        return [
            send(
                gpart.at[q, ((core + dc) % nc) * nx + (x + dx) % nx],
                ga.at[q, e], ga_s.at[q, e], ga_r.at[q, e], peer,
            )
            for e, ((dc, dx), peer) in enumerate(zip(near, npeers))
        ]

    def gram_b(q, copies):
        for c in copies:
            c.wait_recv()
        total = gpart[q, me]
        for e in range(parts - 1):
            total = total + ga[q, e]
        gsum[q] = total
        return [
            send(gsum.at[q], gb.at[q, d], gb_s.at[q, d], gb_r.at[q, d], peer)
            for d, peer in enumerate(ypeers)
        ]

    def gram_c(q, copies):
        for c in copies:
            c.wait_recv()
        total = gsum[q]
        for d in range(ny - 1):
            total = total + gb[q, d]
        gsum2[q] = total
        return [
            send(gsum2.at[q], gc.at[q, d], gc_s.at[q, d], gc_r.at[q, d], peer)
            for d, peer in enumerate(zpeers)
        ]

    def gram_d(q, copies):
        for c in copies:
            c.wait_recv()
        total = gsum2[q]
        for d in range(nz - 1):
            total = total + gc[q, d]
        gfull[q, 0] = total
        return [
            send(gfull.at[q, 0], gfull.at[q, e + 1], gd_s.at[q, e], gd_r.at[q, e], peer)
            for e, peer in enumerate(npeers)
        ]

    def gram_whole(q, copies):
        for c in copies:
            c.wait_recv()
        pieces = [
            gfull[q, ((core + nc - p // nx) % nc) * nx + (x + nx - p % nx) % nx]
            for p in range(parts)
        ]
        return jnp.concatenate(pieces, axis=0)

    narrow = [send(nar, nar_h.at[h], nar_s.at[h], nar_r.at[h], peer) for h, peer in enumerate(sides)]
    sum1 = gram_a(0, smoothed1)
    product(2, 1, nar[...], part2, True)
    for c in narrow:
        c.wait_recv()
    for h in range(2):
        product(h, 2 * h, nar_h[h], part2, False)
    scatter = [
        send(part2.at[(x + d) % nx], rs2.at[d - 1], rs2_s.at[d - 1], rs2_r.at[d - 1], peer)
        for d, peer in zip(range(1, nx), xpeers)
    ]
    sum1 = gram_c(0, gram_b(0, sum1))
    for c in scatter:
        c.wait_recv()
    total = part2[x]
    for d in range(nx - 1):
        total = total + rs2[d]
    smoothed2 = total / degree
    yall[0] = smoothed2
    sum2 = gram_b(1, gram_a(1, smoothed2))
    gather = [
        send(yall.at[0], yall.at[d], y_s.at[d - 1], y_r.at[d - 1], peer)
        for d, peer in zip(range(1, nx), xpeers)
    ]
    sum2 = gram_c(1, sum2)
    first = inverse_factor(gram_whole(0, gram_d(0, sum1)))
    gram = gram_whole(1, gram_d(1, sum2))

    inner = dot_nt(dot_nn(first, gram[:, :K], HIGH), first, HIGH)
    second = inverse_factor(jnp.concatenate([inner, inner], axis=1))
    whiten = dot_nn(second, first, HIGH)
    for c in gather:
        c.wait_recv()
    for p in range(nx):
        out[:, pl.ds(p * block, block)] = dot_nn(whiten, yall[(x + nx - p) % nx], HIGH)
    for c in started:
        c.wait_send()


def solution(mesh):
    nx = mesh.shape["cols"]
    groups = mesh.shape["rows"]
    nz = groups // (NY * NC)
    parts = NC * nx

    def local(embeddings, knn_mean, pair_rows, pair_cols, pair_count, start_block):
        here, width = embeddings.shape
        block = here // nx
        height = K // parts
        dma = pltpu.SemaphoreType.DMA
        vmem = pl.BlockSpec(memory_space=pltpu.VMEM)
        hbm = pl.BlockSpec(memory_space=pl.ANY)
        return pl.pallas_call(
            functools.partial(kernel, nz, NY, NC, nx, here * groups),
            out_shape=jax.ShapeDtypeStruct((K, here), F32),
            in_specs=[hbm, vmem, vmem, vmem, vmem, hbm],
            out_specs=vmem,
            scratch_shapes=[
                pltpu.VMEM((here, width), BF16),
                pltpu.VMEM((here, width), BF16),
                pltpu.VMEM((2, block, width), BF16),
                pltpu.VMEM((block, width), BF16),
                pltpu.VMEM((nx, 8, block), F32),
                pltpu.VMEM((2, 8, block), F32),
                pltpu.VMEM((here, 128), F32),
                pltpu.VMEM((K, block), F32),
                pltpu.VMEM((2, K, block), F32),
                pltpu.VMEM((3, here, block), BF16),
                pltpu.VMEM((nx, KA, block), F32),
                pltpu.VMEM((nx, K, block), BF16),
                pltpu.VMEM((nx, K, block), F32),
                pltpu.VMEM((nx - 1, K, block), BF16),
                pltpu.VMEM((nx - 1, KD - K, block), F32),
                pltpu.VMEM((nx - 1, K, block), F32),
                pltpu.VMEM((K, block), BF16),
                pltpu.VMEM((2, K, block), BF16),
                pltpu.VMEM((3 * nx * nx, 128), F32),
                pltpu.VMEM((nx - 1, 3 * nx * nx, 128), F32),
                pltpu.VMEM((3 * nx * nx, 128), F32),
                pltpu.VMEM((nx, K, block), F32),
                pltpu.VMEM((2, parts, height, 2 * K), F32),
                pltpu.VMEM((2, parts - 1, height, 2 * K), F32),
                pltpu.VMEM((2, height, 2 * K), F32),
                pltpu.VMEM((2, NY - 1, height, 2 * K), F32),
                pltpu.VMEM((2, height, 2 * K), F32),
                pltpu.VMEM((2, nz - 1, height, 2 * K), F32),
                pltpu.VMEM((2, parts, height, 2 * K), F32),
                dma((nx + 1,)),
                dma((2,)), dma((2,)), dma((2,)), dma((2,)), dma((2,)), dma((2,)),
                dma((nx - 1,)), dma((nx - 1,)),
                dma((nx - 1,)), dma((nx - 1,)), dma((nx - 1,)), dma((nx - 1,)),
                dma((nx - 1,)), dma((nx - 1,)),
                dma((2,)), dma((2,)),
                dma((nx - 1,)), dma((nx - 1,)),
                dma((2, parts - 1)), dma((2, parts - 1)),
                dma((2, NY - 1)), dma((2, NY - 1)),
                dma((2, nz - 1)), dma((2, nz - 1)),
                dma((2, parts - 1)), dma((2, parts - 1)),
                pltpu.SemaphoreType.REGULAR((4,)),
            ],
            compiler_params=pltpu.CompilerParams(collective_id=0, has_side_effects=True),
        )(embeddings, knn_mean, pair_rows, pair_cols, pair_count, start_block)

    in_specs = (
        P("rows", None),
        P("rows"),
        P("rows", "cols", None),
        P("rows", "cols", None),
        P("rows", "cols"),
        P(None, "rows"),
    )
    out_specs = P(None, "rows")
    return jax.shard_map(local, mesh=mesh, in_specs=in_specs, out_specs=out_specs, check_vma=False)
```

time: 85.2 us -> 64 us (0.75)
  Pallas kernels: 81.4 us -> 61.5 us
  local copies, waits for them, and re-layouts: 2.95 us -> 1.67 us
    pallas_call x1, Pallas kernels: 81.4 us -> 61.5 us  [local(): pl.pallas_call(functools.partial(kernel, nz, NY, NC, nx, here * groups),...]
    reshape x1 -> x0, local copies, waits for them, and re-layouts: 1.28 us -> none  [local(): knn_mean.reshape(1, here)]
where the time goes in v2:
time: 64 us; the launch traced here: 63.9 us
  Pallas kernels  61.5 us (96%)
  local copies, waits for them, and re-layouts  1.67 us (3%)
  between operations  0.66 us (1%)
    pallas_call x1, Pallas kernels, local(): pl.pallas_call(functools.partial(kernel, nz, NY, NC, nx, here * groups),...  61.5 us
    unnamed x1, local copies, waits for them, and re-layouts  1.67 us

profile of v2, /device:TPU:1, one launch (start us, length us, event | category | flops | bytes accessed | tf_op | source)
XLA Modules:
  0.0 63.9 jit_solution(5853059447977765949)
XLA Ops:
  0.7 61.5 %shard_map.64 = f32[64,1024]{1,0:T(8,128)} custom-call(bf16[1024,1024]{1,0:T(8,128)(2,1)} %emb.1, bf16[1024]{0:T(1024)(128)(2,1)} %knn.1, s32[1,1,24]{2,1,0:T(1,128)} %prow.1, s32[1,1,24]{2,1,0:T(1,128)} %pcol.1, s32[1,1]{1,0:T(1,128)S(6)} %copy.8.pcnt, f32[64,1024]{1,0:T(8,128)} %start.1), custom_call_target="tpu_custom_call" | custom-call | tf_op jit(solution)/shard_map/pallas_call | solution.py:399
  62.2 1.7 %copy.9 = f32[64,1024]{1,0:T(8,128)} copy(f32[64,1024]{1,0:T(8,128)} %shard_map.64) | data formatting | bytes 524288

commit v3 on v2

--- a/solution.py
+++ b/solution.py
@@ -55,6 +55,7 @@
     def spread(values, k):
         return jnp.broadcast_to(values[:, k : k + 1], wide)
 
+    matrix = jnp.concatenate([matrix, matrix], axis=1)
     blocks = [matrix[8 * m : 8 * m + 8, :] for m in range(tall)]
     marks = [lane == row8 + 8 * m for m in range(tall)]
     diagonals = [jnp.where(marks[m], blocks[m], 0.0) for m in range(tall)]
@@ -107,11 +108,11 @@
 
 def kernel(
     nz, ny, nc, nx, total_rows,
-    emb, knn, prow, pcol, pcnt, start,
+    emb, knn_in, prow_in, pcol_in, pcnt_in, start,
     out,
-    emb_v, unit, emb_h, unit_h, km, km_h, mcol, v0, v0_h, aff, part1, half1, part2, rs1, rs1_d, rs2,
+    knn, prow, pcol, pcnt, out_v, emb_v, unit, emb_h, unit_h, km, km_h, mcol, v0, v0_h, aff, part1, half1, part2, rs1, rs1_d, rs2,
     nar, nar_h, mask, mask_x, msum, yall, gpart, ga, gsum, gb, gsum2, gc, gfull,
-    local_sem, emb_s, emb_r, km_s, km_r, v0_s, v0_r, mask_s, mask_r,
+    local_sem, out_sem, emb_s, emb_r, km_s, km_r, v0_s, v0_r, mask_s, mask_r,
     rs1_s, rs1_r, rsd_s, rsd_r, rs2_s, rs2_r, nar_s, nar_r, y_s, y_r,
     ga_s, ga_r, gb_s, gb_r, gc_s, gc_r, gd_s, gd_r, reach_sem,
 ):
@@ -160,7 +161,21 @@
         started.append(copy)
         return copy
 
+    def reach_signal(n):
+        for dz in (rounds[n], -rounds[n]):
+            pl.semaphore_signal(
+                reach_sem.at[n], inc=1, device_id=at(dz=nz + dz), device_id_type=MESH
+            )
+
     own = pl.ds(pl.multiple_of(x * block, block), block)
+    tables = [
+        pltpu.make_async_copy(src, dst, local_sem.at[blocks + 1 + n])
+        for n, (src, dst) in enumerate(
+            ((knn_in, knn), (prow_in, prow), (pcol_in, pcol), (pcnt_in, pcnt))
+        )
+    ]
+    for c in tables:
+        c.start()
     for r in range(blocks):
         pltpu.make_async_copy(
             emb.at[pl.ds(r * block, block)], emb_v.at[pl.ds(r * block, block)], local_sem.at[r]
@@ -168,6 +183,13 @@
     load_v = pltpu.make_async_copy(start.at[:, own], v0, local_sem.at[blocks])
     load_v.start()
 
+    pl.semaphore_wait(barrier, len(everyone))
+
+    for h, peer in enumerate(sides):
+        send(emb.at[own], emb_h.at[h], emb_s.at[h], emb_r.at[h], peer)
+
+    for c in tables:
+        c.wait()
     slots = prow.shape[-1]
     spot = (prow[0] - g * blocks) * (3 * blocks) + (pcol[0] - (g - 1) * blocks)
     live = lax.broadcasted_iota(jnp.int32, (1, slots), 1) < pcnt[...]
@@ -179,25 +201,13 @@
     means = knn[...].astype(F32).reshape(1, here)
     for r in range(blocks):
         km[r] = jnp.broadcast_to(means[:, r * block : (r + 1) * block], (8, block))
-
-    def reach_signal(n):
-        for dz in (rounds[n], -rounds[n]):
-            pl.semaphore_signal(
-                reach_sem.at[n], inc=1, device_id=at(dz=nz + dz), device_id_type=MESH
-            )
-
-    pl.semaphore_wait(barrier, len(everyone))
-
     for h, peer in enumerate(sides):
         send(km.at[x], km_h.at[h], km_s.at[h], km_r.at[h], peer)
-    for h, peer in enumerate(sides):
-        send(emb.at[own], emb_h.at[h], emb_s.at[h], emb_r.at[h], peer)
     for h, peer in enumerate(sides):
         send(start.at[:, own], v0_h.at[h], v0_s.at[h], v0_r.at[h], peer)
     masks = [
         send(mask, mask_x.at[d], mask_s.at[d], mask_r.at[d], peer) for d, peer in enumerate(xpeers)
     ]
-
     if rounds:
         reach_signal(0)
 
@@ -283,12 +293,12 @@
     smoothed1 = total / degree
     nar[...] = smoothed1.astype(BF16)
 
-    height = K // parts
+    height = K // 2 // parts
     me = core * nx + x
 
     def gram_a(q, smoothed):
         gram = dot_nt(smoothed, smoothed, HIGH) * (1.0 / total_rows)
-        gram = jnp.concatenate([gram, jnp.zeros_like(gram)], axis=1)
+        gram = jnp.concatenate([gram[: K // 2], gram[K // 2 :]], axis=1)
         for p in range(parts):
             gpart[q, p] = gram[p * height : (p + 1) * height, :]
         return [
@@ -342,7 +352,8 @@
             gfull[q, ((core + nc - p // nx) % nc) * nx + (x + nx - p % nx) % nx]
             for p in range(parts)
         ]
-        return jnp.concatenate(pieces, axis=0)
+        packed = jnp.concatenate(pieces, axis=0)
+        return jnp.concatenate([packed[:, :K], packed[:, K:]], axis=0)
 
     narrow = [send(nar, nar_h.at[h], nar_s.at[h], nar_r.at[h], peer) for h, peer in enumerate(sides)]
     sum1 = gram_a(0, smoothed1)
@@ -370,17 +381,25 @@
     ]
     sum2 = gram_c(1, sum2)
     first = inverse_factor(gram_whole(0, gram_d(0, sum1)))
-    gram = gram_whole(1, gram_d(1, sum2))
-
-    inner = dot_nt(dot_nn(first, gram[:, :K], HIGH), first, HIGH)
-    second = inverse_factor(jnp.concatenate([inner, inner], axis=1))
-    whiten = dot_nn(second, first, HIGH)
     for c in gather:
         c.wait_recv()
+    once = [dot_nn(first, yall[(x + nx - p) % nx], HIGH) for p in range(nx)]
     for p in range(nx):
-        out[:, pl.ds(p * block, block)] = dot_nn(whiten, yall[(x + nx - p) % nx], HIGH)
+        out_v[p] = once[p]
+    gram = gram_whole(1, gram_d(1, sum2))
+
+    second = inverse_factor(dot_nt(dot_nn(first, gram, HIGH), first, HIGH))
+    stores = []
+    for p in range(nx):
+        out_v[p] = dot_nn(second, out_v[p], HIGH)
+        stores.append(
+            pltpu.make_async_copy(out_v.at[p], out.at[:, pl.ds(p * block, block)], out_sem.at[p])
+        )
+        stores[p].start()
     for c in started:
         c.wait_send()
+    for c in stores:
+        c.wait()
 
 
 def solution(mesh):
@@ -392,16 +411,20 @@
     def local(embeddings, knn_mean, pair_rows, pair_cols, pair_count, start_block):
         here, width = embeddings.shape
         block = here // nx
-        height = K // parts
+        height = K // 2 // parts
         dma = pltpu.SemaphoreType.DMA
-        vmem = pl.BlockSpec(memory_space=pltpu.VMEM)
         hbm = pl.BlockSpec(memory_space=pl.ANY)
         return pl.pallas_call(
             functools.partial(kernel, nz, NY, NC, nx, here * groups),
             out_shape=jax.ShapeDtypeStruct((K, here), F32),
-            in_specs=[hbm, vmem, vmem, vmem, vmem, hbm],
-            out_specs=vmem,
+            in_specs=[hbm] * 6,
+            out_specs=hbm,
             scratch_shapes=[
+                pltpu.VMEM(knn_mean.shape, BF16),
+                pltpu.VMEM(pair_rows.shape, jnp.int32),
+                pltpu.VMEM(pair_cols.shape, jnp.int32),
+                pltpu.VMEM(pair_count.shape, jnp.int32),
+                pltpu.VMEM((nx, K, block), F32),
                 pltpu.VMEM((here, width), BF16),
                 pltpu.VMEM((here, width), BF16),
                 pltpu.VMEM((2, block, width), BF16),
@@ -431,7 +454,7 @@
                 pltpu.VMEM((2, height, 2 * K), F32),
                 pltpu.VMEM((2, nz - 1, height, 2 * K), F32),
                 pltpu.VMEM((2, parts, height, 2 * K), F32),
-                dma((nx + 1,)),
+                dma((nx + 5,)), dma((nx,)),
                 dma((2,)), dma((2,)), dma((2,)), dma((2,)), dma((2,)), dma((2,)),
                 dma((nx - 1,)), dma((nx - 1,)),
                 dma((nx - 1,)), dma((nx - 1,)), dma((nx - 1,)), dma((nx - 1,)),

time: 64 us -> 62.5 us (0.977)
  Pallas kernels: 61.5 us -> 60 us
    pallas_call x1, Pallas kernels: 61.5 us -> 60 us  [local(): pl.pallas_call(functools.partial(kernel, nz, NY, NC, nx, here * groups),...]
where the time goes in v3:
time: 62.5 us; the launch traced here: 62.3 us
  Pallas kernels  60 us (96%)
  local copies, waits for them, and re-layouts  1.67 us (3%)
  between operations  0.66 us (1%)
    pallas_call x1, Pallas kernels, local(): pl.pallas_call(functools.partial(kernel, nz, NY, NC, nx, here * groups),...  60 us
    unnamed x1, local copies, waits for them, and re-layouts  1.67 us

profile of v3, /device:TPU:1, one launch (start us, length us, event | category | flops | bytes accessed | tf_op | source)
XLA Modules:
  0.0 62.3 jit_solution(5717294998703317470)
XLA Ops:
  0.7 60.0 %shard_map.64 = f32[64,1024]{1,0:T(8,128)} custom-call(bf16[1024,1024]{1,0:T(8,128)(2,1)} %emb.1, bf16[1024]{0:T(1024)(128)(2,1)} %knn_in.1, s32[1,1,24]{2,1,0:T(1,128)} %prow_in.1, s32[1,1,24]{2,1,0:T(1,128)} %pcol_in.1, s32[1,1]{1,0:T(1,128)S(6)} %copy.8.pcnt_in, f32[64,1024]{1,0:T(8,128)} %start.1), custom_call_target="tpu_custom_call" | custom-call | tf_op jit(solution)/shard_map/pallas_call | solution.py:417
  60.6 1.7 %copy.9 = f32[64,1024]{1,0:T(8,128)} copy(f32[64,1024]{1,0:T(8,128)} %shard_map.64) | data formatting | bytes 524288

commit v4 on v3

--- a/solution.py
+++ b/solution.py
@@ -131,7 +131,9 @@
         row = (((z + dz) % nz) * ny + (y + dy) % ny) * nc + (core + dc) % nc
         return (row, (x + dx) % nx)
 
-    sides = [((g + 1) % rows, x), ((g + rows - 1) % rows, x)]
+    sides = [((g + rows + 2 * core - 1) % rows, x), ((g + rows + 1 - 2 * core) % rows, x)]
+    lands = [1 - core, core]
+    comes = [core, 1 - core]
     near = [(e // nx, e % nx) for e in range(1, parts)]
     xpeers = [at(dx=d) for d in range(1, nx)]
     npeers = [at(dc=dc, dx=dx) for dc, dx in near]
@@ -185,7 +187,7 @@
 
     pl.semaphore_wait(barrier, len(everyone))
 
-    for h, peer in enumerate(sides):
+    for h, peer in zip(lands, sides):
         send(emb.at[own], emb_h.at[h], emb_s.at[h], emb_r.at[h], peer)
 
     for c in tables:
@@ -201,9 +203,9 @@
     means = knn[...].astype(F32).reshape(1, here)
     for r in range(blocks):
         km[r] = jnp.broadcast_to(means[:, r * block : (r + 1) * block], (8, block))
-    for h, peer in enumerate(sides):
+    for h, peer in zip(lands, sides):
         send(km.at[x], km_h.at[h], km_s.at[h], km_r.at[h], peer)
-    for h, peer in enumerate(sides):
+    for h, peer in zip(lands, sides):
         send(start.at[:, own], v0_h.at[h], v0_s.at[h], v0_r.at[h], peer)
     masks = [
         send(mask, mask_x.at[d], mask_s.at[d], mask_r.at[d], peer) for d, peer in enumerate(xpeers)
@@ -233,13 +235,20 @@
                 weights = jnp.where((lane == line) & (x == r), 0.0, weights)
             aff[slot, rows_at, :] = weights.astype(BF16)
 
-    def product(slot, window, source, part, first):
-        for r in range(blocks):
-            live_pair = msum[pl.ds(r * 3 * blocks + window * blocks + x, 1), :][:, 0:1]
-            piece = dot_nt(source, aff[slot, pl.ds(r * block, block), :]) * live_pair
-            part[r, pl.ds(0, piece.shape[0]), :] = (
-                piece if first else part[r, pl.ds(0, piece.shape[0]), :] + piece
-            )
+    order = sorted(range(nx), key=lambda d: -min(d, nx - d))
+
+    def product(slot, window, source, part, first, finish=None):
+        height = source.shape[0]
+        for d in order:
+            p = (x + d) % nx
+            live_pair = msum[pl.ds(p * 3 * blocks + window * blocks + x, 1), :][:, 0:1]
+            rows_at = pl.ds(pl.multiple_of(p * block, block), block)
+            piece = dot_nt(source, aff[slot, rows_at, :]) * live_pair
+            if not first:
+                piece = part[p, pl.ds(0, height), :] + piece
+            part[p, pl.ds(0, height), :] = piece
+            if finish is not None and d > 0:
+                finish(d, p, piece)
 
     tail = lax.broadcasted_iota(jnp.int32, (KA - K, block), 0)
     ones = jnp.where(tail == 0, 1.0, 0.0)
@@ -261,27 +270,25 @@
         if n + 1 < len(rounds):
             reach_signal(n + 1)
 
-    def side(step, carry):
-        h = (core + 1 + step) % 2
+    scatter = []
+
+    def scatter1(d, p, values):
+        e, peer = d - 1, xpeers[d - 1]
+        half1[p] = values[:K].astype(BF16)
+        scatter.append(send(half1.at[p], rs1.at[e], rs1_s.at[e], rs1_r.at[e], peer))
+        scatter.append(
+            send(part1.at[p, pl.ds(K, KD - K)], rs1_d.at[e], rsd_s.at[e], rsd_r.at[e], peer)
+        )
+
+    for n in (1, 0):
+        h = comes[n]
         remote(km.at[x], km_h.at[h], km_s.at[h], km_r.at[h], sides[0]).wait_recv()
         remote(emb.at[own], emb_h.at[h], emb_s.at[h], emb_r.at[h], sides[0]).wait_recv()
         normalize(emb_h.at[h], unit_h, block)
         affinity(h, unit_h[...], km_h[h, 0:1, :], False)
         remote(start.at[:, own], v0_h.at[h], v0_s.at[h], v0_r.at[h], sides[0]).wait_recv()
-        product(h, 2 * h, widened(v0_h[h]), part1, False)
-        return carry
-
-    lax.fori_loop(0, 2, side, 0)
-
-    for r in range(blocks):
-        half1[r] = part1[r, pl.ds(0, K), :].astype(BF16)
-    scatter = []
-    for d, peer in zip(range(1, nx), xpeers):
-        p, e = (x + d) % nx, d - 1
-        scatter.append(send(half1.at[p], rs1.at[e], rs1_s.at[e], rs1_r.at[e], peer))
-        scatter.append(
-            send(part1.at[p, pl.ds(K, KD - K)], rs1_d.at[e], rsd_s.at[e], rsd_r.at[e], peer)
-        )
+        product(h, 2 * h, widened(v0_h[h]), part1, False, None if n else scatter1)
+
     for c in scatter:
         c.wait_recv()
     total = part1[x, pl.ds(0, K), :]
@@ -330,7 +337,7 @@
         gsum2[q] = total
         return [
             send(gsum2.at[q], gc.at[q, d], gc_s.at[q, d], gc_r.at[q, d], peer)
-            for d, peer in enumerate(zpeers)
+            for d, peer in sorted(enumerate(zpeers), key=lambda item: -min(item[0] + 1, nz - item[0] - 1))
         ]
 
     def gram_d(q, copies):
@@ -355,17 +362,20 @@
         packed = jnp.concatenate(pieces, axis=0)
         return jnp.concatenate([packed[:, :K], packed[:, K:]], axis=0)
 
-    narrow = [send(nar, nar_h.at[h], nar_s.at[h], nar_r.at[h], peer) for h, peer in enumerate(sides)]
+    for h, peer in zip(lands, sides):
+        send(nar, nar_h.at[h], nar_s.at[h], nar_r.at[h], peer)
     sum1 = gram_a(0, smoothed1)
     product(2, 1, nar[...], part2, True)
-    for c in narrow:
-        c.wait_recv()
-    for h in range(2):
-        product(h, 2 * h, nar_h[h], part2, False)
-    scatter = [
-        send(part2.at[(x + d) % nx], rs2.at[d - 1], rs2_s.at[d - 1], rs2_r.at[d - 1], peer)
-        for d, peer in zip(range(1, nx), xpeers)
-    ]
+    scatter = []
+
+    def scatter2(d, p, values):
+        e = d - 1
+        scatter.append(send(part2.at[p], rs2.at[e], rs2_s.at[e], rs2_r.at[e], xpeers[e]))
+
+    for n in (1, 0):
+        h = comes[n]
+        remote(nar, nar_h.at[h], nar_s.at[h], nar_r.at[h], sides[0]).wait_recv()
+        product(h, 2 * h, nar_h[h], part2, False, None if n else scatter2)
     sum1 = gram_c(0, gram_b(0, sum1))
     for c in scatter:
         c.wait_recv()

time: 62.5 us -> 62.5 us (level)
  no operation moved by 1% of the time
where the time goes in v4:
time: 62.5 us; the launch traced here: 62.4 us
  Pallas kernels  60.1 us (96%)
  local copies, waits for them, and re-layouts  1.67 us (3%)
  between operations  0.66 us (1%)
    pallas_call x1, Pallas kernels, local(): pl.pallas_call(functools.partial(kernel, nz, NY, NC, nx, here * groups),...  60.1 us
    unnamed x1, local copies, waits for them, and re-layouts  1.67 us

profile of v4, /device:TPU:1, one launch (start us, length us, event | category | flops | bytes accessed | tf_op | source)
XLA Modules:
  0.0 62.4 jit_solution(3022506378819048241)
XLA Ops:
  0.7 60.1 %shard_map.64 = f32[64,1024]{1,0:T(8,128)} custom-call(bf16[1024,1024]{1,0:T(8,128)(2,1)} %emb.1, bf16[1024]{0:T(1024)(128)(2,1)} %knn_in.1, s32[1,1,24]{2,1,0:T(1,128)} %prow_in.1, s32[1,1,24]{2,1,0:T(1,128)} %pcol_in.1, s32[1,1]{1,0:T(1,128)S(6)} %copy.8.pcnt_in, f32[64,1024]{1,0:T(8,128)} %start.1), custom_call_target="tpu_custom_call" | custom-call | tf_op jit(solution)/shard_map/pallas_call | solution.py:427
  60.7 1.7 %copy.9 = f32[64,1024]{1,0:T(8,128)} copy(f32[64,1024]{1,0:T(8,128)} %shard_map.64) | data formatting | bytes 524288
